TPU v7x, 256 devices: a whole 4x4x8 slice. The times are simulated.
256 devices in a mesh: frames: 4 (over y_lo, core), lon: 64 (over y_hi, x, z).
Axes of the slice: x: 4, y: 4 (y_hi: 2, y_lo: 2; y = y_hi * 2 + y_lo), z: 8, core: 2. Of those that a mesh axis runs over, the one named last changes fastest.
Arguments:
- latents: bfloat16 [32, 2, 1024, 1024], P('frames', None, 'lon'), may hold values from -30 to 30
- window_weight: int32 [32, 64], P('frames'), may hold values from 1 to 8
- modulation: float32 [6, 1024], replicated, may hold values from -4 to 4
- query_spatial: bfloat16 [1024, 512], replicated, may hold values from -2 to 2, as said below
- key_spatial: bfloat16 [1024, 512], replicated, may hold values from -2 to 2, as said below
- value_spatial: bfloat16 [1024, 512], replicated, may hold values from -0.1875 to 0.1875
- out_spatial: bfloat16 [512, 1024], replicated, may hold values from -0.25 to 0.25
- query_temporal: bfloat16 [1024, 512], replicated, may hold values from -2 to 2, as said below
- key_temporal: bfloat16 [1024, 512], replicated, may hold values from -2 to 2, as said below
- value_temporal: bfloat16 [1024, 512], replicated, may hold values from -0.1875 to 0.1875
- out_temporal: bfloat16 [512, 1024], replicated, may hold values from -0.25 to 0.25
Outputs:
- block_output: bfloat16 [32, 2, 1024, 1024], P('frames', None, 'lon')
Inputs may be any that keep to these rules, and one draw needn't show every extreme that they name: `query_spatial`: entries of a projection. `key_spatial`: entries of a projection. `query_temporal`: entries of a projection. `key_temporal`: entries of a projection.
All inputs are finite; a program needn't handle non-finite values.
Results may differ from a plain program's by a relative error of at most 0.0065.
Values may be sent and summed in bfloat16 or wider, within the bound.
No kernel may reach another device: no remote copies, remote signals or barrier semaphores. Data moves between devices by JAX's collectives and lax.ppermute only.
A program may use at most 64 MiB of HBM per device.

v0:
```python
import functools

import jax
import jax.numpy as jnp
from jax import lax
from jax.experimental import pallas as pl
from jax.experimental.pallas import tpu as pltpu
from jax.sharding import PartitionSpec as P


HEADS = 8
HD = 64
D = 1024
HW = 512
F = 8
SPOTS = 32
TOK = F * SPOTS
PIECES = (5, 3)
STARTS = tuple(sum(PIECES[:i]) for i in range(len(PIECES)))
GROUP = 8
GROUPS = SPOTS // GROUP
LANES = 128
TOGETHER = 16
SPACE_TOGETHER = 16
AHEAD = True
PAD = True
EPSILON = 1e-06
NEG = -1e30
MIB = 1024 * 1024


VM = pl.BlockSpec(memory_space=pltpu.VMEM)
HBM = pl.BlockSpec(memory_space=pltpu.HBM)


def f32dot(a, b):
    return jnp.dot(a, b, preferred_element_type=jnp.float32)


def project(a, w_ref):
    return f32dot(a, w_ref[...]).astype(jnp.bfloat16)


def scaled(q):
    return (q * HD**-0.5).astype(jnp.bfloat16)


def normed(values, shift_row, scale_row):
    centre = jnp.mean(values, axis=-1, keepdims=True)
    centred = values - centre
    spread = jnp.mean(centred * centred, axis=-1, keepdims=True)
    return (centred * lax.rsqrt(spread + EPSILON)) * (1.0 + scale_row) + shift_row


def spread_heads(q, count):
    head = lax.broadcasted_iota(jnp.int32, q.shape, 1) // HD
    zero = jnp.zeros_like(q)
    return jnp.concatenate([jnp.where(head == h, q, zero) for h in range(count)], axis=0)


def gather_heads(o, rows, count):
    tiles = []
    half = lax.broadcasted_iota(jnp.int32, (rows, LANES), 1) < HD
    for tile in range(count * HD // LANES):
        lanes = slice(tile * LANES, (tile + 1) * LANES)
        even = o[2 * tile * rows : (2 * tile + 1) * rows, lanes]
        odd = o[(2 * tile + 1) * rows : (2 * tile + 2) * rows, lanes]
        tiles.append(jnp.where(half, even, odd))
    return tiles[0] if len(tiles) == 1 else jnp.concatenate(tiles, axis=1)


def raise_scores(keys, stacked, n, bias=None):
    scores = lax.dot_general(
        keys, stacked, (((1,), (1,)), ((), ())), preferred_element_type=jnp.float32
    )
    out = []
    for i in range(keys.shape[0] // n):
        part = scores[i * n : (i + 1) * n]
        if bias is not None:
            part = part + bias
        top = jnp.max(part, axis=0, keepdims=True)
        raised = jnp.exp(part - top)
        out.append((raised, top, jnp.sum(raised, axis=0, keepdims=True)))
    return out


def window_factors(share, first, second):
    high = jnp.maximum(first[0], second[0])
    a, b = jnp.exp(first[0] - high), jnp.exp(second[0] - high)
    scale = share / (first[1] * a + second[1] * b)
    return a * scale, b * scale


def mix_values(raised, factors, values, rows, count):
    weights = jnp.concatenate(
        [(part * factor).astype(jnp.bfloat16) for part, factor in zip(raised, factors)], axis=0
    )
    mix = lax.dot_general(
        weights,
        jnp.concatenate(values, axis=0),
        (((0,), (0,)), ((), ())),
        preferred_element_type=jnp.float32,
    )
    return gather_heads(mix, rows, count)


def split_kernel(x_ref, *refs):
    for ref, start, frames in zip(refs, STARTS, PIECES):
        ref[...] = x_ref[start * SPOTS : (start + frames) * SPOTS]


def own_kernel(*refs):
    mod_ref, weight_ref, x_hbm, wq_hbm = refs[:4]
    stored_hbm = refs[4:11]
    share_ref, x_ref, q_ref, kv_ref = refs[11:15]
    stored = refs[15:22]
    wq_ref, sem = refs[22:]
    copies = [
        pltpu.make_async_copy(src, dst, sem.at[i])
        for i, (src, dst) in enumerate(
            zip((x_hbm, wq_hbm) + stored_hbm, (x_ref, wq_ref) + stored)
        )
    ]
    for copy in copies:
        copy.start()

    count = weight_ref.shape[1]
    strip = lax.axis_index("lon")
    weights = weight_ref[...].astype(jnp.float32)
    spot = lax.broadcasted_iota(jnp.int32, weights.shape, 1)
    here = jnp.sum(jnp.where(spot == strip, weights, 0.0), axis=1, keepdims=True)
    prior = jnp.sum(
        jnp.where(spot == lax.rem(strip + count - 1, count), weights, 0.0), axis=1, keepdims=True
    )
    near = jnp.where(lax.rem(strip, 2) == 0, here, prior)
    share_ref[...] = jnp.broadcast_to(near / (here + prior), share_ref.shape)

    copies[0].wait()
    n = normed(x_ref[...].astype(jnp.float32), mod_ref[0:1], mod_ref[1:2]).astype(jnp.bfloat16)
    copies[1].wait()
    q_ref[...] = scaled(project(n, wq_ref))
    for i in range(2):
        copies[2 + i].wait()
        kv_ref[:, i * HW : (i + 1) * HW] = project(n, stored[i])
    for copy in copies[4:]:
        copy.wait()


def quad_lanes(quad):
    wide = HW // 2
    return slice(quad * wide, (quad + 1) * wide), slice(HW + quad * wide, HW + (quad + 1) * wide)


def frame_rows(f):
    return slice(f * SPOTS, (f + 1) * SPOTS)


def near_kernel(x_ref, share_ref, q_ref, kv_ref, mod_ref, wk_ref, wv_ref, part_ref, raised_ref, stats_ref):
    n = normed(x_ref[...].astype(jnp.float32), mod_ref[0:1], mod_ref[1:2]).astype(jnp.bfloat16)
    k_near, v_near = project(n, wk_ref), project(n, wv_ref)
    units = [(f, quad) for f in range(F) for quad in range(2)]
    for first in range(0, len(units), SPACE_TOGETHER):
        batch = units[first : first + SPACE_TOGETHER]
        scored = []
        for f, quad in batch:
            lanes, after = quad_lanes(quad)
            at = frame_rows(f)
            keys = jnp.concatenate([kv_ref[at, lanes], k_near[at, lanes]], axis=0)
            stacked = spread_heads(q_ref[at, lanes], HEADS // 2)
            scored.append(raise_scores(keys, stacked, SPOTS))
        for (f, quad), (own, other) in zip(batch, scored):
            lanes, after = quad_lanes(quad)
            at = frame_rows(f)
            unit = 2 * f + quad
            raised_ref[unit] = own[0]
            stats_ref[unit, 0:1] = own[1]
            stats_ref[unit, 1:2] = own[2]
            part_ref[at, lanes] = mix_values(
                [own[0], other[0]],
                window_factors(share_ref[f : f + 1], own[1:], other[1:]),
                [kv_ref[at, after], v_near[at, lanes]],
                SPOTS,
                HEADS // 2,
            )


def space_kernel(start, frames, *refs):
    far_ref, part_ref, raised_ref, stats_ref, share_ref, x_ref, q_ref, kv_ref = refs[:8]
    mod_ref, wk_ref, wv_ref, wo_ref, wkt_ref, wvt_ref = refs[8:14]
    mixed_ref, n_ref, kvt_ref = refs[14:]
    rows = frames * SPOTS
    far = far_ref[...]
    if PAD and rows < LANES:
        far = jnp.concatenate([far, far[: LANES - rows]], axis=0)
    n = normed(far.astype(jnp.float32), mod_ref[0:1], mod_ref[1:2]).astype(jnp.bfloat16)
    k_far, v_far = project(n, wk_ref), project(n, wv_ref)
    units = [(f, quad) for f in range(frames) for quad in range(2)]
    blended = {}
    for first in range(0, len(units), SPACE_TOGETHER):
        batch = units[first : first + SPACE_TOGETHER]
        scored = []
        for f, quad in batch:
            lanes, after = quad_lanes(quad)
            stacked = spread_heads(q_ref[frame_rows(start + f), lanes], HEADS // 2)
            scored += raise_scores(k_far[frame_rows(f), lanes], stacked, SPOTS)
        for (f, quad), other in zip(batch, scored):
            lanes, after = quad_lanes(quad)
            own = frame_rows(start + f)
            unit = 2 * (start + f) + quad
            stats = (stats_ref[unit, 0:1], stats_ref[unit, 1:2])
            share = 1.0 - share_ref[start + f : start + f + 1]
            mix = mix_values(
                [raised_ref[unit], other[0]],
                window_factors(share, stats, other[1:]),
                [kv_ref[own, after], v_far[frame_rows(f), lanes]],
                SPOTS,
                HEADS // 2,
            )
            blended[f, quad] = (part_ref[own, lanes] + mix).astype(jnp.bfloat16)
    blended = jnp.concatenate(
        [
            jnp.concatenate([blended[f, quad] for quad in range(2)], axis=1)
            for f in range(frames)
        ],
        axis=0,
    )
    here = slice(start * SPOTS, (start + frames) * SPOTS)
    branch = f32dot(blended, wo_ref[...])
    mixed = (x_ref[here].astype(jnp.float32) + mod_ref[2:3] * branch).astype(jnp.bfloat16)
    mixed_ref[...] = mixed
    n = normed(mixed.astype(jnp.float32), mod_ref[3:4], mod_ref[4:5])
    n = n.reshape(frames, GROUPS, GROUP, D).transpose(1, 0, 2, 3).reshape(rows, D)
    n = n.astype(jnp.bfloat16)
    kvt_ref[:, :HW] = project(n, wkt_ref)
    kvt_ref[:, HW:] = project(n, wvt_ref)
    n_ref[...] = n


def time_setup():
    rows = F * GROUP
    key_spot = lax.broadcasted_iota(jnp.int32, (rows, LANES), 0) % GROUP
    query_spot = lax.broadcasted_iota(jnp.int32, (rows, LANES), 1) % GROUP
    bias = jnp.where(key_spot == query_spot, 0.0, NEG)
    group = lax.axis_index("frames")
    inner = jnp.logical_and(group > 0, group < lax.axis_size("frames") - 1)
    return bias, jnp.where(inner, 0.5, 0.0)


def rows_of(refs, g, lanes):
    return jnp.concatenate(
        [
            ref[g * frames * GROUP : (g + 1) * frames * GROUP, lanes]
            for ref, frames in zip(refs, PIECES)
        ],
        axis=0,
    )


def pair_lanes(pair):
    return slice(pair * LANES, (pair + 1) * LANES), slice(
        HW + pair * LANES, HW + (pair + 1) * LANES
    )


def mate_kernel(*refs):
    count = len(PIECES)
    wq_ref = refs[0]
    n_refs, own_refs, mate_refs = (refs[1 + i * count : 1 + (i + 1) * count] for i in range(3))
    q_ref, part_ref, raised_ref, stats_ref = refs[1 + 3 * count :]
    bias, paired = time_setup()
    n = F * GROUP
    q = scaled(project(jnp.concatenate([ref[...] for ref in n_refs], axis=0), wq_ref))
    for g in range(GROUPS):
        q_ref[g * n : (g + 1) * n] = jnp.concatenate(
            [
                q[start * SPOTS + g * frames * GROUP : start * SPOTS + (g + 1) * frames * GROUP]
                for start, frames in zip(STARTS, PIECES)
            ],
            axis=0,
        )
    units = [(g, pair) for g in range(GROUPS) for pair in range(HEADS // 2)]
    for first in range(0, len(units), TOGETHER):
        batch = units[first : first + TOGETHER]
        scored = []
        for g, pair in batch:
            lanes, after = pair_lanes(pair)
            stacked = spread_heads(q_ref[g * n : (g + 1) * n, lanes], 2)
            keys = jnp.concatenate(
                [rows_of(own_refs, g, lanes), rows_of(mate_refs, g, lanes)], axis=0
            )
            scored.append(raise_scores(keys, stacked, n, bias))
        for (g, pair), (own, other) in zip(batch, scored):
            lanes, after = pair_lanes(pair)
            unit = g * (HEADS // 2) + pair
            raised_ref[unit] = own[0]
            stats_ref[unit, 0:1] = own[1]
            stats_ref[unit, 1:2] = own[2]
            part_ref[g * n : (g + 1) * n, lanes] = mix_values(
                [own[0], other[0]],
                window_factors(1.0 - paired, own[1:], other[1:]),
                [rows_of(own_refs, g, after), rows_of(mate_refs, g, after)],
                n,
                2,
            )


def cross_kernel(mod_ref, wo_ref, q_ref, part_ref, raised_ref, stats_ref, *refs):
    count = len(PIECES)
    own_refs, cross_refs, mixed_refs = (refs[i * count : (i + 1) * count] for i in range(3))
    out_hbm, out_ref, sem = refs[3 * count :]
    bias, paired = time_setup()
    n = F * GROUP
    copies = []
    per = GROUPS // 2
    pairs = range(HEADS // 2)

    def score(half):
        scored = {}
        for g in range(half * per, (half + 1) * per):
            for pair in pairs:
                lanes, _ = pair_lanes(pair)
                stacked = spread_heads(q_ref[g * n : (g + 1) * n, lanes], 2)
                scored[g, pair] = raise_scores(rows_of(cross_refs, g, lanes), stacked, n, bias)[0]
        return scored

    scored = {}
    if AHEAD:
        for half in range(2):
            scored.update(score(half))
    for half in range(2):
        if not AHEAD:
            scored = score(half)
        rows = []
        for g in range(half * per, (half + 1) * per):
            row = []
            for pair in pairs:
                lanes, after = pair_lanes(pair)
                unit = g * (HEADS // 2) + pair
                other = scored[g, pair]
                stats = (stats_ref[unit, 0:1], stats_ref[unit, 1:2])
                mix = mix_values(
                    [raised_ref[unit], other[0]],
                    window_factors(paired, stats, other[1:]),
                    [rows_of(own_refs, g, after), rows_of(cross_refs, g, after)],
                    n,
                    2,
                )
                row.append((part_ref[g * n : (g + 1) * n, lanes] + mix).astype(jnp.bfloat16))
            rows.append(jnp.concatenate(row, axis=1))
        branch = mod_ref[5:6] * f32dot(jnp.concatenate(rows, axis=0), wo_ref[...])
        branch = branch.reshape(per, F, GROUP, D)
        spots = pl.ds(half * per, per)
        for mixed_ref, start, frames in zip(mixed_refs, STARTS, PIECES):
            for f in range(frames):
                for i in range(per):
                    at = f * SPOTS + (half * per + i) * GROUP
                    mixed = mixed_ref[at : at + GROUP].astype(jnp.float32)
                    out_ref[start + f, half * per + i] = (mixed + branch[i, start + f]).astype(
                        jnp.bfloat16
                    )
        for f in range(0, F, 2):
            pick = pl.ds(f, 2)
            copies.append(
                pltpu.make_async_copy(
                    out_ref.at[pick, spots], out_hbm.at[pick, spots], sem.at[half * F + f]
                )
            )
            copies[-1].start()
    for copy in copies:
        copy.wait()


def body(
    latents,
    window_weight,
    modulation,
    query_spatial,
    key_spatial,
    value_spatial,
    out_spatial,
    query_temporal,
    key_temporal,
    value_temporal,
    out_temporal,
):
    strips = lax.axis_size("lon")
    groups = lax.axis_size("frames")
    bf = jnp.bfloat16
    shape = jax.ShapeDtypeStruct
    params = pltpu.CompilerParams

    def keep(array):
        return pltpu.with_memory_space_constraint(array, pltpu.HBM)

    x = latents.reshape(TOK, D)
    near_pairs = [(i, i ^ 1) for i in range(strips)]
    far_pairs = [(i, (i + (1 if i % 2 else -1)) % strips) for i in range(strips)]
    mates = [(i, i ^ 1) for i in range(groups)]
    crossing = []
    for i in range(groups):
        for s in range(strips):
            if i in (0, groups - 1):
                crossing.append((i * strips + s, i * strips + (s ^ 1)))
            else:
                partner = i + 1 if i % 2 else i - 1
                crossing.append((i * strips + s, partner * strips + s))

    near = lax.ppermute(x, "lon", near_pairs)
    pieces = pl.pallas_call(
        split_kernel,
        out_shape=[shape((n * SPOTS, D), bf) for n in PIECES],
        in_specs=[VM],
        out_specs=[VM] * len(PIECES),
        compiler_params=params(vmem_limit_bytes=4 * MIB),
        name="split",
    )(x)
    far = []
    for piece in pieces:
        far.append(lax.ppermute(piece, "lon", far_pairs))

    wide, tall = shape((D, HW), bf), shape((HW, D), bf)
    stored = pl.pallas_call(
        own_kernel,
        out_shape=[shape((F, LANES), jnp.float32), shape((TOK, D), bf)]
        + [shape((TOK, HW), bf), shape((TOK, D), bf)]
        + [wide, wide, tall, wide, wide, wide, tall],
        in_specs=[VM] * 2 + [HBM] * 9,
        out_specs=[VM] * 11,
        scratch_shapes=[pltpu.VMEM((D, HW), bf), pltpu.SemaphoreType.DMA((9,))],
        compiler_params=params(vmem_limit_bytes=24 * MIB),
        name="own",
    )(
        modulation,
        window_weight,
        *map(
            keep,
            (
                x,
                query_spatial,
                key_spatial,
                value_spatial,
                out_spatial,
                key_temporal,
                value_temporal,
                query_temporal,
                out_temporal,
            ),
        ),
    )
    share, own_x, q, kv = stored[:4]
    weights = stored[4:9]
    space_units = 2 * F
    near_parts = pl.pallas_call(
        near_kernel,
        out_shape=[
            shape((TOK, HW), jnp.float32),
            shape((space_units, SPOTS, LANES), jnp.float32),
            shape((space_units, 8, LANES), jnp.float32),
        ],
        in_specs=[VM] * 7,
        out_specs=[VM] * 3,
        compiler_params=params(vmem_limit_bytes=16 * MIB),
        name="near",
    )(near, share, q, kv, modulation, *weights[:2])
    time_args = []
    for i, (start, frames) in enumerate(zip(STARTS, PIECES)):
        rows = frames * SPOTS
        args = (far[i], *near_parts, share, own_x, q, kv, modulation, *weights)
        mixed, nt, kvt = pl.pallas_call(
            functools.partial(space_kernel, start, frames),
            out_shape=[shape((rows, D), bf)] * 3,
            in_specs=[VM] * len(args),
            out_specs=[VM] * 3,
            compiler_params=params(vmem_limit_bytes=20 * MIB),
        )(*args)
        cross = lax.ppermute(kvt, ("frames", "lon"), crossing)
        mate = lax.ppermute(kvt, "frames", mates)
        time_args.append((nt, kvt, mate, cross, mixed))

    nts, kvts, mate_kvs, cross_kvs, mixeds = zip(*time_args)
    units = GROUPS * HEADS // 2
    parts = pl.pallas_call(
        mate_kernel,
        out_shape=[
            shape((TOK, HW), bf),
            shape((TOK, HW), jnp.float32),
            shape((units, F * GROUP, LANES), jnp.float32),
            shape((units, 8, LANES), jnp.float32),
        ],
        in_specs=[VM] * (1 + 3 * len(PIECES)),
        out_specs=[VM] * 4,
        compiler_params=params(vmem_limit_bytes=12 * MIB),
        name="timea",
    )(stored[9], *nts, *kvts, *mate_kvs)
    out_shape = (F, GROUPS, GROUP, D)
    out = pl.pallas_call(
        cross_kernel,
        out_shape=shape(out_shape, bf),
        in_specs=[VM] * (6 + 3 * len(PIECES)),
        out_specs=HBM,
        scratch_shapes=[pltpu.VMEM(out_shape, bf), pltpu.SemaphoreType.DMA((2 * F,))],
        compiler_params=params(vmem_limit_bytes=16 * MIB),
        name="timeb",
    )(modulation, stored[10], *parts, *kvts, *cross_kvs, *mixeds)
    return out.reshape(latents.shape)


def solution(mesh):
    return jax.shard_map(
        body,
        mesh=mesh,
        in_specs=(P("frames", None, "lon", None), P("frames", None)) + (P(),) * 9,
        out_specs=P("frames", None, "lon", None),
        check_vma=False,
    )
```

profile of v0, /device:TPU:1, one launch (start us, length us, event | category | flops | bytes accessed | tf_op | source)
XLA Modules:
  0.0 35.6 jit_solution(61653821947151093)
XLA Ops:
  0.0 2.5 %collective-permute-start.1 = (bf16[256,1024]{1,0:T(8,128)(2,1)}, bf16[256,1024]{1,0:T(8,128)(2,1)S(1)}, u32[]{:S(2)}, u32[]{:S(2)}) collective-permute-start(bf16[256,1024]{1,0:T(8,128)(2,1)} %bitcast.2), channel_id=1, source_target_pairs={{0,1},{1,0},{2,3},{3,2},{4,5},{5,4},{6,7},{7,6},{8,9},{9,8},{10,11... | collective-permute-start | bytes 1572872 | tf_op jit(solution)/shard_map/ppermute | solution.py:408
  2.5 0.0 copy-start
  2.5 1.1 %copy-done = bf16[8,2,16,1024]{3,2,1,0:T(8,128)(2,1)S(1)} copy-done((bf16[8,2,16,1024]{3,2,1,0:T(8,128)(2,1)S(1)}, bf16[8,2,16,1024]{3,2,1,0:T(8,128)(2,1)}, u32[]{:S(2)}) %copy-start) | copy-done | bytes 524312
  3.5 0.0 copy-start.1
  3.5 0.0 copy-start.2
  3.6 9.6 %collective-permute-start = (bf16[160,1024]{1,0:T(8,128)(2,1)S(1)}, bf16[160,1024]{1,0:T(8,128)(2,1)S(1)}, u32[]{:S(2)}, u32[]{:S(2)}) collective-permute-start(bf16[160,1024]{1,0:T(8,128)(2,1)S(1)} %get-tuple-element.33), channel_id=1, source_target_pairs={{0,63},{1,2},{2,1},{3,4},{4,3},{5,6},{6,5},{7,8},{8,7},{9,10},{10,... | collective-permute-start | bytes 983048 | tf_op jit(solution)/shard_map/ppermute | solution.py:419
  13.2 0.1 collective-permute-start.2
  13.3 0.0 copy-done.1
  13.3 0.0 copy-done.2
  13.3 3.6 %own.1 = (f32[8,128]{1,0:T(8,128)S(1)}, bf16[256,1024]{1,0:T(8,128)(2,1)S(1)}, bf16[256,512]{1,0:T(8,128)(2,1)S(1)}, bf16[256,1024]{1,0:T(8,128)(2,1)S(1)}, bf16...) custom-call(f32[6,1024]{1,0:T(8,128)S(1)} %copy-done.1, ...), custom_call_target="tpu_custom_call" | custom-call | tf_op jit(solution)/shard_map/own/pallas_call | solution.py:422
  16.9 0.0 collective-permute-done.1.x_ref
  16.9 1.6 %near.1 = (f32[256,512]{1,0:T(8,128)S(1)}, f32[16,32,128]{2,1,0:T(8,128)S(1)}, f32[16,8,128]{2,1,0:T(8,128)S(1)}) custom-call(bf16[256,1024]{1,0:T(8,128)(2,1)S(1)} %collective-permute-done.1.x_ref, f32[8,128]{1,0:T(8,128)S(1)} %get-tuple-element.34.share_ref.refs_4_, bf16[256,512]{1,0:T(8,128)(2,1)S(1)} %get-tuple-element.35.q_ref.refs_6_, ...), custom_call_target="tpu_custom_call" | custom-call | tf_op jit(solution)/shard_map/near/pallas_call | solution.py:453
  18.5 1.8 %collective-permute-done.refs_0_ = bf16[160,1024]{1,0:T(8,128)(2,1)S(1)} collective-permute-done((bf16[160,1024]{1,0:T(8,128)(2,1)S(1)}, bf16[160,1024]{1,0:T(8,128)(2,1)S(1)}, u32[]{:S(2)}, u32[]{:S(2)}) %collective-permute-start) | collective-permute-done | bytes 327712 | tf_op jit(solution)/shard_map/ppermute | solution.py:419
  20.3 2.1 %shard_map.109 = (bf16[160,1024]{1,0:T(8,128)(2,1)S(1)}, bf16[160,1024]{1,0:T(8,128)(2,1)S(1)}, bf16[160,1024]{1,0:T(8,128)(2,1)S(1)}) custom-call(bf16[160,1024]{1,0:T(8,128)(2,1)S(1)} %collective-permute-done.refs_0_, f32[256,512]{1,0:T(8,128)S(1)} %get-tuple-element.39.refs_1_, f32[16,32,128]{2,1,0:T(8,128)S(1)} %get-tuple-element.40.refs_2_, ...), custom_call_target="tpu_custom_call" | custom-call | tf_op jit(solution)/shard_map/pallas_call | solution.py:469
  22.4 2.3 %collective-permute-start.3 = (bf16[160,1024]{1,0:T(8,128)(2,1)S(1)}, bf16[160,1024]{1,0:T(8,128)(2,1)S(1)}, u32[]{:S(2)}, u32[]{:S(2)}) collective-permute-start(bf16[160,1024]{1,0:T(8,128)(2,1)S(1)} %get-tuple-element.49.refs_3_.refs_0_), channel_id=1, source_target_pairs={{0,64},{64,0},{128,192},{192,128},{1,65},{65,1},{129,193},{193,129... | collective-permute-start | bytes 983048 | tf_op jit(solution)/shard_map/ppermute | solution.py:477
  24.7 0.4 %collective-permute-start.5 = (bf16[160,1024]{1,0:T(8,128)(2,1)S(1)}, bf16[160,1024]{1,0:T(8,128)(2,1)S(1)}, u32[]{:S(2)}, u32[]{:S(2)}) collective-permute-start(bf16[160,1024]{1,0:T(8,128)(2,1)S(1)} %get-tuple-element.49.refs_3_.refs_0_), channel_id=1, source_target_pairs={{0,1},{1,0},{2,3},{3,2},{4,5},{5,4},{6,7},{7,6},{8,9},{9,8},{10,11... | collective-permute-start | bytes 983048 | tf_op jit(solution)/shard_map/ppermute | solution.py:476
  25.1 0.0 collective-permute-done.2.refs_0_
  25.1 1.9 %shard_map.110 = (bf16[96,1024]{1,0:T(8,128)(2,1)S(1)}, bf16[96,1024]{1,0:T(8,128)(2,1)S(1)}, bf16[96,1024]{1,0:T(8,128)(2,1)S(1)}) custom-call(bf16[96,1024]{1,0:T(8,128)(2,1)S(1)} %collective-permute-done.2.refs_0_, f32[256,512]{1,0:T(8,128)S(1)} %get-tuple-element.39.refs_1_, f32[16,32,128]{2,1,0:T(8,128)S(1)} %get-tuple-element.40.refs_2_, ...), custom_call_target="tpu_custom_call" | custom-call | tf_op jit(solution)/shard_map/pallas_call | solution.py:469
  27.0 1.2 %collective-permute-start.4 = (bf16[96,1024]{1,0:T(8,128)(2,1)S(1)}, bf16[96,1024]{1,0:T(8,128)(2,1)S(1)}, u32[]{:S(2)}, u32[]{:S(2)}) collective-permute-start(bf16[96,1024]{1,0:T(8,128)(2,1)S(1)} %get-tuple-element.50.refs_4_.refs_1_), channel_id=1, source_target_pairs={{0,64},{64,0},{128,192},{192,128},{1,65},{65,1},{129,193},{193,129... | collective-permute-start | bytes 589832 | tf_op jit(solution)/shard_map/ppermute | solution.py:477
  28.2 0.4 %collective-permute-start.6 = (bf16[96,1024]{1,0:T(8,128)(2,1)S(1)}, bf16[96,1024]{1,0:T(8,128)(2,1)S(1)}, u32[]{:S(2)}, u32[]{:S(2)}) collective-permute-start(bf16[96,1024]{1,0:T(8,128)(2,1)S(1)} %get-tuple-element.50.refs_4_.refs_1_), channel_id=1, source_target_pairs={{0,1},{1,0},{2,3},{3,2},{4,5},{5,4},{6,7},{7,6},{8,9},{9,8},{10,11... | collective-permute-start | bytes 589832 | tf_op jit(solution)/shard_map/ppermute | solution.py:476
  28.5 0.7 %collective-permute-done.4.refs_6_ = bf16[96,1024]{1,0:T(8,128)(2,1)S(1)} collective-permute-done((bf16[96,1024]{1,0:T(8,128)(2,1)S(1)}, bf16[96,1024]{1,0:T(8,128)(2,1)S(1)}, u32[]{:S(2)}, u32[]{:S(2)}) %collective-permute-start.4) | collective-permute-done | bytes 196640 | tf_op jit(solution)/shard_map/ppermute | solution.py:477
  29.2 0.0 collective-permute-done.3.refs_5_
  29.2 1.3 %timea.1 = (bf16[256,512]{1,0:T(8,128)(2,1)S(1)}, f32[256,512]{1,0:T(8,128)S(1)}, f32[16,64,128]{2,1,0:T(8,128)S(1)}, f32[16,8,128]{2,1,0:T(8,128)S(1)}) custom-call(bf16[1024,512]{1,0:T(8,128)(2,1)S(1)} %get-tuple-element.32.refs_0_, bf16[160,1024]{1,0:T(8,128)(2,1)S(1)} %get-tuple-element.46.refs_1_, bf16[96,1024]{1,0:T(8,128)(2,1)S(1)} %get-tuple-element.48.refs_2_, ...), custom_call_target="tpu_custom_call" | custom-call | tf_op jit(solution)/shard_map/timea/pallas_call | solution.py:482
  30.5 3.1 %collective-permute-done.6.refs_3_ = bf16[96,1024]{1,0:T(8,128)(2,1)S(1)} collective-permute-done((bf16[96,1024]{1,0:T(8,128)(2,1)S(1)}, bf16[96,1024]{1,0:T(8,128)(2,1)S(1)}, u32[]{:S(2)}, u32[]{:S(2)}) %collective-permute-start.6) | collective-permute-done | bytes 196640 | tf_op jit(solution)/shard_map/ppermute | solution.py:476
  33.6 0.0 collective-permute-done.5.refs_2_
  33.6 2.0 %timeb.1 = bf16[8,4,8,1024]{3,2,1,0:T(8,128)(2,1)} custom-call(f32[6,1024]{1,0:T(8,128)S(1)} %copy-done.1, bf16[512,1024]{1,0:T(8,128)(2,1)S(1)} %get-tuple-element.31.wo_ref, bf16[256,512]{1,0:T(8,128)(2,1)S(1)} %get-tuple-element.51.q_ref, f32[256,512]{1,0:T(8,128)S(1)} %get-tuple-element.52.part_ref, f32[16,64,128]{2,1,0:T(8,128)S(1)} %get-tuple-element.53.raised_ref, ...), custom_call_target="tpu_custom_call" | custom-call | tf_op jit(solution)/shard_map/timeb/pallas_call | solution.py:496
  (1 shorter events, 0.0 us)
Async XLA Ops:
  0.0 16.9 %collective-permute-start.1 = (bf16[256,1024]{1,0:T(8,128)(2,1)}, bf16[256,1024]{1,0:T(8,128)(2,1)S(1)}, u32[]{:S(2)}, u32[]{:S(2)}) collective-permute-start(bf16[256,1024]{1,0:T(8,128)(2,1)} %bitcast.2), channel_id=1, source_target_pairs={{0,1},{1,0},{2,3},{3,2},{4,5},{5,4},{6,7},{7,6},{8,9},{9,8},{10,11... | collective-permute-start | bytes 1572872 | tf_op jit(solution)/shard_map/ppermute | solution.py:408
  2.5 1.1 %copy-start = (bf16[8,2,16,1024]{3,2,1,0:T(8,128)(2,1)S(1)}, bf16[8,2,16,1024]{3,2,1,0:T(8,128)(2,1)}, u32[]{:S(2)}) copy-start(bf16[8,2,16,1024]{3,2,1,0:T(8,128)(2,1)} %param.11) | copy-start | bytes 1572868
  3.5 9.7 %copy-start.1 = (f32[6,1024]{1,0:T(8,128)S(1)}, f32[6,1024]{1,0:T(8,128)}, u32[]{:S(2)}) copy-start(f32[6,1024]{1,0:T(8,128)} %mod_ref.3) | copy-start | bytes 73732
  3.5 9.7 %copy-start.2 = (s32[8,64]{1,0:T(8,128)S(1)}, s32[8,64]{1,0:T(8,128)}, u32[]{:S(2)}) copy-start(s32[8,64]{1,0:T(8,128)} %refs_1_.1) | copy-start | bytes 6148
  3.6 16.7 %collective-permute-start = (bf16[160,1024]{1,0:T(8,128)(2,1)S(1)}, bf16[160,1024]{1,0:T(8,128)(2,1)S(1)}, u32[]{:S(2)}, u32[]{:S(2)}) collective-permute-start(bf16[160,1024]{1,0:T(8,128)(2,1)S(1)} %get-tuple-element.33), channel_id=1, source_target_pairs={{0,63},{1,2},{2,1},{3,4},{4,3},{5,6},{6,5},{7,8},{8,7},{9,10},{10,... | collective-permute-start | bytes 983048 | tf_op jit(solution)/shard_map/ppermute | solution.py:419
  13.2 11.9 %collective-permute-start.2 = (bf16[96,1024]{1,0:T(8,128)(2,1)S(1)}, bf16[96,1024]{1,0:T(8,128)(2,1)S(1)}, u32[]{:S(2)}, u32[]{:S(2)}) collective-permute-start(bf16[96,1024]{1,0:T(8,128)(2,1)S(1)} %get-tuple-element.47), channel_id=1, source_target_pairs={{0,63},{1,2},{2,1},{3,4},{4,3},{5,6},{6,5},{7,8},{8,7},{9,10},{10,... | collective-permute-start | bytes 589832 | tf_op jit(solution)/shard_map/ppermute | solution.py:419
  22.4 6.8 %collective-permute-start.3 = (bf16[160,1024]{1,0:T(8,128)(2,1)S(1)}, bf16[160,1024]{1,0:T(8,128)(2,1)S(1)}, u32[]{:S(2)}, u32[]{:S(2)}) collective-permute-start(bf16[160,1024]{1,0:T(8,128)(2,1)S(1)} %get-tuple-element.49.refs_3_.refs_0_), channel_id=1, source_target_pairs={{0,64},{64,0},{128,192},{192,128},{1,65},{65,1},{129,193},{193,129... | collective-permute-start | bytes 983048 | tf_op jit(solution)/shard_map/ppermute | solution.py:477
  24.7 8.9 %collective-permute-start.5 = (bf16[160,1024]{1,0:T(8,128)(2,1)S(1)}, bf16[160,1024]{1,0:T(8,128)(2,1)S(1)}, u32[]{:S(2)}, u32[]{:S(2)}) collective-permute-start(bf16[160,1024]{1,0:T(8,128)(2,1)S(1)} %get-tuple-element.49.refs_3_.refs_0_), channel_id=1, source_target_pairs={{0,1},{1,0},{2,3},{3,2},{4,5},{5,4},{6,7},{7,6},{8,9},{9,8},{10,11... | collective-permute-start | bytes 983048 | tf_op jit(solution)/shard_map/ppermute | solution.py:476
  27.0 2.3 %collective-permute-start.4 = (bf16[96,1024]{1,0:T(8,128)(2,1)S(1)}, bf16[96,1024]{1,0:T(8,128)(2,1)S(1)}, u32[]{:S(2)}, u32[]{:S(2)}) collective-permute-start(bf16[96,1024]{1,0:T(8,128)(2,1)S(1)} %get-tuple-element.50.refs_4_.refs_1_), channel_id=1, source_target_pairs={{0,64},{64,0},{128,192},{192,128},{1,65},{65,1},{129,193},{193,129... | collective-permute-start | bytes 589832 | tf_op jit(solution)/shard_map/ppermute | solution.py:477
  28.2 5.4 %collective-permute-start.6 = (bf16[96,1024]{1,0:T(8,128)(2,1)S(1)}, bf16[96,1024]{1,0:T(8,128)(2,1)S(1)}, u32[]{:S(2)}, u32[]{:S(2)}) collective-permute-start(bf16[96,1024]{1,0:T(8,128)(2,1)S(1)} %get-tuple-element.50.refs_4_.refs_1_), channel_id=1, source_target_pairs={{0,1},{1,0},{2,3},{3,2},{4,5},{5,4},{6,7},{7,6},{8,9},{9,8},{10,11... | collective-permute-start | bytes 589832 | tf_op jit(solution)/shard_map/ppermute | solution.py:476
where the time goes:
time: 35.8 us; the launch traced here: 35.6 us
  starting transfers between devices  16.4 us (46%)
  Pallas kernels  12.6 us (35%)
  waiting for transfers between devices  5.55 us (16%)
  local copies, waits for them, and re-layouts  1.08 us (3%)
    ppermute x2, starting transfers between devices, body(): far.append(lax.ppermute(piece, 'lon', far_pairs))  9.68 us
    pallas_call x2, Pallas kernels, body(): pl.pallas_call(functools.partial(space_kernel, start, frames), out_shape=...  4 us
    pallas_call x1, Pallas kernels, body(): pl.pallas_call(own_kernel, out_shape=[shape((F, LANES), jnp.float32), sha...  3.64 us
    ppermute x2, starting transfers between devices, body(): mate = lax.ppermute(kvt, 'frames', mates)  3.48 us
    ppermute x2, waiting for transfers between devices, body(): cross = lax.ppermute(kvt, ('frames', 'lon'), crossing)  3.1 us
    ppermute x1, starting transfers between devices, body(): near = lax.ppermute(x, 'lon', near_pairs)  2.46 us
    pallas_call x1, Pallas kernels, body(): pl.pallas_call(cross_kernel, out_shape=shape(out_shape, bf), in_specs=[VM...  2.04 us
    ppermute x2, waiting for transfers between devices, body(): far.append(lax.ppermute(piece, 'lon', far_pairs))  1.75 us
  transfers between devices with their start and end apart: 7, of which 3 were waited for; matrix products, arithmetic and copies ran while one was open for 0% of the time, Pallas kernels for 30%

commit v1 on v0

--- a/solution.py
+++ b/solution.py
@@ -358,14 +358,10 @@
                     out_ref[start + f, half * per + i] = (mixed + branch[i, start + f]).astype(
                         jnp.bfloat16
                     )
-        for f in range(0, F, 2):
-            pick = pl.ds(f, 2)
-            copies.append(
-                pltpu.make_async_copy(
-                    out_ref.at[pick, spots], out_hbm.at[pick, spots], sem.at[half * F + f]
-                )
-            )
-            copies[-1].start()
+        copies.append(
+            pltpu.make_async_copy(out_ref.at[:, spots], out_hbm.at[:, spots], sem.at[half])
+        )
+        copies[-1].start()
     for copy in copies:
         copy.wait()
 
@@ -498,7 +494,7 @@
         out_shape=shape(out_shape, bf),
         in_specs=[VM] * (6 + 3 * len(PIECES)),
         out_specs=HBM,
-        scratch_shapes=[pltpu.VMEM(out_shape, bf), pltpu.SemaphoreType.DMA((2 * F,))],
+        scratch_shapes=[pltpu.VMEM(out_shape, bf), pltpu.SemaphoreType.DMA((2,))],
         compiler_params=params(vmem_limit_bytes=16 * MIB),
         name="timeb",
     )(modulation, stored[10], *parts, *kvts, *cross_kvs, *mixeds)

time: 35.8 us -> 35.7 us (level)
  no operation moved by 1% of the time
where the time goes in v1:
time: 35.7 us; the launch traced here: 35.5 us
  starting transfers between devices  16.4 us (46%)
  Pallas kernels  12.5 us (35%)
  waiting for transfers between devices  5.55 us (16%)
  local copies, waits for them, and re-layouts  1.08 us (3%)
    ppermute x2, starting transfers between devices, body(): far.append(lax.ppermute(piece, 'lon', far_pairs))  9.68 us
    pallas_call x2, Pallas kernels, body(): pl.pallas_call(functools.partial(space_kernel, start, frames), out_shape=...  4 us
    pallas_call x1, Pallas kernels, body(): pl.pallas_call(own_kernel, out_shape=[shape((F, LANES), jnp.float32), sha...  3.64 us
    ppermute x2, starting transfers between devices, body(): mate = lax.ppermute(kvt, 'frames', mates)  3.48 us
    ppermute x2, waiting for transfers between devices, body(): cross = lax.ppermute(kvt, ('frames', 'lon'), crossing)  3.1 us
    ppermute x1, starting transfers between devices, body(): near = lax.ppermute(x, 'lon', near_pairs)  2.46 us
    pallas_call x1, Pallas kernels, body(): pl.pallas_call(cross_kernel, out_shape=shape(out_shape, bf), in_specs=[VM...  1.93 us
    ppermute x2, waiting for transfers between devices, body(): far.append(lax.ppermute(piece, 'lon', far_pairs))  1.75 us
  transfers between devices with their start and end apart: 7, of which 3 were waited for; matrix products, arithmetic and copies ran while one was open for 0% of the time, Pallas kernels for 30%

profile of v1, /device:TPU:1, one launch (start us, length us, event | category | flops | bytes accessed | tf_op | source)
XLA Modules:
  0.0 35.5 jit_solution(10149621918974573895)
XLA Ops:
  0.0 2.5 %collective-permute-start.1 = (bf16[256,1024]{1,0:T(8,128)(2,1)}, bf16[256,1024]{1,0:T(8,128)(2,1)S(1)}, u32[]{:S(2)}, u32[]{:S(2)}) collective-permute-start(bf16[256,1024]{1,0:T(8,128)(2,1)} %bitcast.2), channel_id=1, source_target_pairs={{0,1},{1,0},{2,3},{3,2},{4,5},{5,4},{6,7},{7,6},{8,9},{9,8},{10,11... | collective-permute-start | bytes 1572872 | tf_op jit(solution)/shard_map/ppermute | solution.py:404
  2.5 0.0 copy-start
  2.5 1.1 %copy-done = bf16[8,2,16,1024]{3,2,1,0:T(8,128)(2,1)S(1)} copy-done((bf16[8,2,16,1024]{3,2,1,0:T(8,128)(2,1)S(1)}, bf16[8,2,16,1024]{3,2,1,0:T(8,128)(2,1)}, u32[]{:S(2)}) %copy-start) | copy-done | bytes 524312
  3.5 0.0 copy-start.1
  3.5 0.0 copy-start.2
  3.6 9.6 %collective-permute-start = (bf16[160,1024]{1,0:T(8,128)(2,1)S(1)}, bf16[160,1024]{1,0:T(8,128)(2,1)S(1)}, u32[]{:S(2)}, u32[]{:S(2)}) collective-permute-start(bf16[160,1024]{1,0:T(8,128)(2,1)S(1)} %get-tuple-element.33), channel_id=1, source_target_pairs={{0,63},{1,2},{2,1},{3,4},{4,3},{5,6},{6,5},{7,8},{8,7},{9,10},{10,... | collective-permute-start | bytes 983048 | tf_op jit(solution)/shard_map/ppermute | solution.py:415
  13.2 0.1 collective-permute-start.2
  13.3 0.0 copy-done.1
  13.3 0.0 copy-done.2
  13.3 3.6 %own.1 = (f32[8,128]{1,0:T(8,128)S(1)}, bf16[256,1024]{1,0:T(8,128)(2,1)S(1)}, bf16[256,512]{1,0:T(8,128)(2,1)S(1)}, bf16[256,1024]{1,0:T(8,128)(2,1)S(1)}, bf16...) custom-call(f32[6,1024]{1,0:T(8,128)S(1)} %copy-done.1, ...), custom_call_target="tpu_custom_call" | custom-call | tf_op jit(solution)/shard_map/own/pallas_call | solution.py:418
  16.9 0.0 collective-permute-done.1.x_ref
  16.9 1.6 %near.1 = (f32[256,512]{1,0:T(8,128)S(1)}, f32[16,32,128]{2,1,0:T(8,128)S(1)}, f32[16,8,128]{2,1,0:T(8,128)S(1)}) custom-call(bf16[256,1024]{1,0:T(8,128)(2,1)S(1)} %collective-permute-done.1.x_ref, f32[8,128]{1,0:T(8,128)S(1)} %get-tuple-element.34.share_ref.refs_4_, bf16[256,512]{1,0:T(8,128)(2,1)S(1)} %get-tuple-element.35.q_ref.refs_6_, ...), custom_call_target="tpu_custom_call" | custom-call | tf_op jit(solution)/shard_map/near/pallas_call | solution.py:449
  18.5 1.8 %collective-permute-done.refs_0_ = bf16[160,1024]{1,0:T(8,128)(2,1)S(1)} collective-permute-done((bf16[160,1024]{1,0:T(8,128)(2,1)S(1)}, bf16[160,1024]{1,0:T(8,128)(2,1)S(1)}, u32[]{:S(2)}, u32[]{:S(2)}) %collective-permute-start) | collective-permute-done | bytes 327712 | tf_op jit(solution)/shard_map/ppermute | solution.py:415
  20.3 2.1 %shard_map.109 = (bf16[160,1024]{1,0:T(8,128)(2,1)S(1)}, bf16[160,1024]{1,0:T(8,128)(2,1)S(1)}, bf16[160,1024]{1,0:T(8,128)(2,1)S(1)}) custom-call(bf16[160,1024]{1,0:T(8,128)(2,1)S(1)} %collective-permute-done.refs_0_, f32[256,512]{1,0:T(8,128)S(1)} %get-tuple-element.39.refs_1_, f32[16,32,128]{2,1,0:T(8,128)S(1)} %get-tuple-element.40.refs_2_, ...), custom_call_target="tpu_custom_call" | custom-call | tf_op jit(solution)/shard_map/pallas_call | solution.py:465
  22.4 2.3 %collective-permute-start.3 = (bf16[160,1024]{1,0:T(8,128)(2,1)S(1)}, bf16[160,1024]{1,0:T(8,128)(2,1)S(1)}, u32[]{:S(2)}, u32[]{:S(2)}) collective-permute-start(bf16[160,1024]{1,0:T(8,128)(2,1)S(1)} %get-tuple-element.49.refs_3_.refs_0_), channel_id=1, source_target_pairs={{0,64},{64,0},{128,192},{192,128},{1,65},{65,1},{129,193},{193,129... | collective-permute-start | bytes 983048 | tf_op jit(solution)/shard_map/ppermute | solution.py:473
  24.7 0.4 %collective-permute-start.5 = (bf16[160,1024]{1,0:T(8,128)(2,1)S(1)}, bf16[160,1024]{1,0:T(8,128)(2,1)S(1)}, u32[]{:S(2)}, u32[]{:S(2)}) collective-permute-start(bf16[160,1024]{1,0:T(8,128)(2,1)S(1)} %get-tuple-element.49.refs_3_.refs_0_), channel_id=1, source_target_pairs={{0,1},{1,0},{2,3},{3,2},{4,5},{5,4},{6,7},{7,6},{8,9},{9,8},{10,11... | collective-permute-start | bytes 983048 | tf_op jit(solution)/shard_map/ppermute | solution.py:472
  25.1 0.0 collective-permute-done.2.refs_0_
  25.1 1.9 %shard_map.110 = (bf16[96,1024]{1,0:T(8,128)(2,1)S(1)}, bf16[96,1024]{1,0:T(8,128)(2,1)S(1)}, bf16[96,1024]{1,0:T(8,128)(2,1)S(1)}) custom-call(bf16[96,1024]{1,0:T(8,128)(2,1)S(1)} %collective-permute-done.2.refs_0_, f32[256,512]{1,0:T(8,128)S(1)} %get-tuple-element.39.refs_1_, f32[16,32,128]{2,1,0:T(8,128)S(1)} %get-tuple-element.40.refs_2_, ...), custom_call_target="tpu_custom_call" | custom-call | tf_op jit(solution)/shard_map/pallas_call | solution.py:465
  27.0 1.2 %collective-permute-start.4 = (bf16[96,1024]{1,0:T(8,128)(2,1)S(1)}, bf16[96,1024]{1,0:T(8,128)(2,1)S(1)}, u32[]{:S(2)}, u32[]{:S(2)}) collective-permute-start(bf16[96,1024]{1,0:T(8,128)(2,1)S(1)} %get-tuple-element.50.refs_4_.refs_1_), channel_id=1, source_target_pairs={{0,64},{64,0},{128,192},{192,128},{1,65},{65,1},{129,193},{193,129... | collective-permute-start | bytes 589832 | tf_op jit(solution)/shard_map/ppermute | solution.py:473
  28.2 0.4 %collective-permute-start.6 = (bf16[96,1024]{1,0:T(8,128)(2,1)S(1)}, bf16[96,1024]{1,0:T(8,128)(2,1)S(1)}, u32[]{:S(2)}, u32[]{:S(2)}) collective-permute-start(bf16[96,1024]{1,0:T(8,128)(2,1)S(1)} %get-tuple-element.50.refs_4_.refs_1_), channel_id=1, source_target_pairs={{0,1},{1,0},{2,3},{3,2},{4,5},{5,4},{6,7},{7,6},{8,9},{9,8},{10,11... | collective-permute-start | bytes 589832 | tf_op jit(solution)/shard_map/ppermute | solution.py:472
  28.5 0.7 %collective-permute-done.4.refs_6_ = bf16[96,1024]{1,0:T(8,128)(2,1)S(1)} collective-permute-done((bf16[96,1024]{1,0:T(8,128)(2,1)S(1)}, bf16[96,1024]{1,0:T(8,128)(2,1)S(1)}, u32[]{:S(2)}, u32[]{:S(2)}) %collective-permute-start.4) | collective-permute-done | bytes 196640 | tf_op jit(solution)/shard_map/ppermute | solution.py:473
  29.2 0.0 collective-permute-done.3.refs_5_
  29.2 1.3 %timea.1 = (bf16[256,512]{1,0:T(8,128)(2,1)S(1)}, f32[256,512]{1,0:T(8,128)S(1)}, f32[16,64,128]{2,1,0:T(8,128)S(1)}, f32[16,8,128]{2,1,0:T(8,128)S(1)}) custom-call(bf16[1024,512]{1,0:T(8,128)(2,1)S(1)} %get-tuple-element.32.refs_0_, bf16[160,1024]{1,0:T(8,128)(2,1)S(1)} %get-tuple-element.46.refs_1_, bf16[96,1024]{1,0:T(8,128)(2,1)S(1)} %get-tuple-element.48.refs_2_, ...), custom_call_target="tpu_custom_call" | custom-call | tf_op jit(solution)/shard_map/timea/pallas_call | solution.py:478
  30.5 3.1 %collective-permute-done.6.refs_3_ = bf16[96,1024]{1,0:T(8,128)(2,1)S(1)} collective-permute-done((bf16[96,1024]{1,0:T(8,128)(2,1)S(1)}, bf16[96,1024]{1,0:T(8,128)(2,1)S(1)}, u32[]{:S(2)}, u32[]{:S(2)}) %collective-permute-start.6) | collective-permute-done | bytes 196640 | tf_op jit(solution)/shard_map/ppermute | solution.py:472
  33.6 0.0 collective-permute-done.5.refs_2_
  33.6 1.9 %timeb.1 = bf16[8,4,8,1024]{3,2,1,0:T(8,128)(2,1)} custom-call(f32[6,1024]{1,0:T(8,128)S(1)} %copy-done.1, bf16[512,1024]{1,0:T(8,128)(2,1)S(1)} %get-tuple-element.31.wo_ref, bf16[256,512]{1,0:T(8,128)(2,1)S(1)} %get-tuple-element.51.q_ref, f32[256,512]{1,0:T(8,128)S(1)} %get-tuple-element.52.part_ref, f32[16,64,128]{2,1,0:T(8,128)S(1)} %get-tuple-element.53.raised_ref, ...), custom_call_target="tpu_custom_call" | custom-call | tf_op jit(solution)/shard_map/timeb/pallas_call | solution.py:492
  (1 shorter events, 0.0 us)
Async XLA Ops:
  0.0 16.9 %collective-permute-start.1 = (bf16[256,1024]{1,0:T(8,128)(2,1)}, bf16[256,1024]{1,0:T(8,128)(2,1)S(1)}, u32[]{:S(2)}, u32[]{:S(2)}) collective-permute-start(bf16[256,1024]{1,0:T(8,128)(2,1)} %bitcast.2), channel_id=1, source_target_pairs={{0,1},{1,0},{2,3},{3,2},{4,5},{5,4},{6,7},{7,6},{8,9},{9,8},{10,11... | collective-permute-start | bytes 1572872 | tf_op jit(solution)/shard_map/ppermute | solution.py:404
  2.5 1.1 %copy-start = (bf16[8,2,16,1024]{3,2,1,0:T(8,128)(2,1)S(1)}, bf16[8,2,16,1024]{3,2,1,0:T(8,128)(2,1)}, u32[]{:S(2)}) copy-start(bf16[8,2,16,1024]{3,2,1,0:T(8,128)(2,1)} %param.11) | copy-start | bytes 1572868
  3.5 9.7 %copy-start.1 = (f32[6,1024]{1,0:T(8,128)S(1)}, f32[6,1024]{1,0:T(8,128)}, u32[]{:S(2)}) copy-start(f32[6,1024]{1,0:T(8,128)} %mod_ref.3) | copy-start | bytes 73732
  3.5 9.7 %copy-start.2 = (s32[8,64]{1,0:T(8,128)S(1)}, s32[8,64]{1,0:T(8,128)}, u32[]{:S(2)}) copy-start(s32[8,64]{1,0:T(8,128)} %refs_1_.1) | copy-start | bytes 6148
  3.6 16.7 %collective-permute-start = (bf16[160,1024]{1,0:T(8,128)(2,1)S(1)}, bf16[160,1024]{1,0:T(8,128)(2,1)S(1)}, u32[]{:S(2)}, u32[]{:S(2)}) collective-permute-start(bf16[160,1024]{1,0:T(8,128)(2,1)S(1)} %get-tuple-element.33), channel_id=1, source_target_pairs={{0,63},{1,2},{2,1},{3,4},{4,3},{5,6},{6,5},{7,8},{8,7},{9,10},{10,... | collective-permute-start | bytes 983048 | tf_op jit(solution)/shard_map/ppermute | solution.py:415
  13.2 11.9 %collective-permute-start.2 = (bf16[96,1024]{1,0:T(8,128)(2,1)S(1)}, bf16[96,1024]{1,0:T(8,128)(2,1)S(1)}, u32[]{:S(2)}, u32[]{:S(2)}) collective-permute-start(bf16[96,1024]{1,0:T(8,128)(2,1)S(1)} %get-tuple-element.47), channel_id=1, source_target_pairs={{0,63},{1,2},{2,1},{3,4},{4,3},{5,6},{6,5},{7,8},{8,7},{9,10},{10,... | collective-permute-start | bytes 589832 | tf_op jit(solution)/shard_map/ppermute | solution.py:415
  22.4 6.8 %collective-permute-start.3 = (bf16[160,1024]{1,0:T(8,128)(2,1)S(1)}, bf16[160,1024]{1,0:T(8,128)(2,1)S(1)}, u32[]{:S(2)}, u32[]{:S(2)}) collective-permute-start(bf16[160,1024]{1,0:T(8,128)(2,1)S(1)} %get-tuple-element.49.refs_3_.refs_0_), channel_id=1, source_target_pairs={{0,64},{64,0},{128,192},{192,128},{1,65},{65,1},{129,193},{193,129... | collective-permute-start | bytes 983048 | tf_op jit(solution)/shard_map/ppermute | solution.py:473
  24.7 8.9 %collective-permute-start.5 = (bf16[160,1024]{1,0:T(8,128)(2,1)S(1)}, bf16[160,1024]{1,0:T(8,128)(2,1)S(1)}, u32[]{:S(2)}, u32[]{:S(2)}) collective-permute-start(bf16[160,1024]{1,0:T(8,128)(2,1)S(1)} %get-tuple-element.49.refs_3_.refs_0_), channel_id=1, source_target_pairs={{0,1},{1,0},{2,3},{3,2},{4,5},{5,4},{6,7},{7,6},{8,9},{9,8},{10,11... | collective-permute-start | bytes 983048 | tf_op jit(solution)/shard_map/ppermute | solution.py:472
  27.0 2.3 %collective-permute-start.4 = (bf16[96,1024]{1,0:T(8,128)(2,1)S(1)}, bf16[96,1024]{1,0:T(8,128)(2,1)S(1)}, u32[]{:S(2)}, u32[]{:S(2)}) collective-permute-start(bf16[96,1024]{1,0:T(8,128)(2,1)S(1)} %get-tuple-element.50.refs_4_.refs_1_), channel_id=1, source_target_pairs={{0,64},{64,0},{128,192},{192,128},{1,65},{65,1},{129,193},{193,129... | collective-permute-start | bytes 589832 | tf_op jit(solution)/shard_map/ppermute | solution.py:473
  28.2 5.4 %collective-permute-start.6 = (bf16[96,1024]{1,0:T(8,128)(2,1)S(1)}, bf16[96,1024]{1,0:T(8,128)(2,1)S(1)}, u32[]{:S(2)}, u32[]{:S(2)}) collective-permute-start(bf16[96,1024]{1,0:T(8,128)(2,1)S(1)} %get-tuple-element.50.refs_4_.refs_1_), channel_id=1, source_target_pairs={{0,1},{1,0},{2,3},{3,2},{4,5},{5,4},{6,7},{7,6},{8,9},{9,8},{10,11... | collective-permute-start | bytes 589832 | tf_op jit(solution)/shard_map/ppermute | solution.py:472
